TPU v7x, 32 devices: a whole 2x2x4 slice. The times are simulated.
32 devices in a mesh: area: 8 (over z, x), row: 4 (over y, core).
Axes of the slice: x: 2, y: 2, z: 4, core: 2. Of those that a mesh axis runs over, the one named last changes fastest.
Arguments:
- conductance_inverse: float32 [32, 1024, 1024], P(('area', 'row')), as said below
- cap_history: float32 [32, 1024, 128], P(('area', 'row')), may hold values from -3 to 3
- cap_conductance: float32 [32, 1024], P(('area', 'row')), may hold values from 0.5 to 0.8
- wave_history: float32 [32, 40, 32, 128], P(('area', 'row')), may hold values from -6 to 6
- line_partner: int32 [32, 32], P(('area', 'row')), may hold values from 0 to 31, as said below
- line_node: int32 [32, 32], P(('area', 'row')), may hold values from 0 to 1023
- line_delay: int32 [32, 32], P(('area', 'row')), may hold values from 20 to 40
- line_admittance: float32 [32, 32], P(('area', 'row')), may hold values from 0.2 to 1
- conv_node: int32 [32, 64], P(('area', 'row')), may hold values from 0 to 1023
- conv_count: int32 [32], P(('area', 'row')), may hold values from 1 to 64, as said below
- conv_state: float32 [32, 2, 64, 128], P(('area', 'row')), may hold values from -3 to 3
- conv_reference: float32 [32, 2, 64, 128], P(('area', 'row')), may hold values from -4 to 4
- conv_rate: float32 [32, 64], P(('area', 'row')), may hold values from 0.03 to 0.6
- conv_limit: float32 [32, 64], P(('area', 'row')), may hold values from 1 to 2.5
- port_node: int32 [32, 8], P(('area', 'row')), may hold values from 0 to 1023
- port_admittance: float32 [32, 8], P(('area', 'row')), may hold values from 0.3 to 1.2
- port_voltage_prev: float32 [2, 32, 8, 128], P(None, ('area', 'row')), may hold values from -5 to 5
- port_bus: int32 [32, 8], P('area'), may hold values from 0 to 20479
- transfer_impedance: float32 [2, 20480, 256], P(None, 'row', 'area'), may hold values from -0.75 to 0.75
Outputs:
- waves: float32 [32, 20, 32, 128], P(('area', 'row'))
- cap_history_out: float32 [32, 1024, 128], P(('area', 'row'))
- conv_state_out: float32 [32, 2, 64, 128], P(('area', 'row'))
- bus_voltage: float32 [2, 20480, 128], P(None, 'row')
- port_voltage: float32 [2, 32, 8, 128], P(None, ('area', 'row'))
Inputs may be any that keep to these rules, and one draw needn't show every extreme that they name: Slot l < 16 of subnetwork s and slot l + 16 of subnetwork (s + k_l) mod 32 are the two ends of one line, with k_l in 1 or 2 the same for every subnetwork and exactly 12 of the k_l equal to 1; so line_partner[s, l] = (s + k_l) mod 32 and line_partner[s, l + 16] = (s - k_l) mod 32. `conv_count`: some subnetwork has all 64 converters in service. `conductance_inverse`: each subnetwork's inverse nodal conductance matrix.
All inputs are finite; a program needn't handle non-finite values.
Results may differ from a plain program's by a relative error of at most 0.0003.
Values sent between devices are 32-bit elements; how exact they have to be, the bound alone decides.
A program may use at most 64 MiB of HBM per device.

v0:
```python
import math
import jax
import jax.numpy as jnp
from jax import lax
from jax.sharding import PartitionSpec as P

STEPS = 20
HIST = 40
NEAR = 12
HIGHEST = lax.Precision.HIGHEST
SAG_FACTOR = 0.3


def from_behind(x, axis, by):
    size = lax.axis_size(axis)
    return lax.ppermute(x, axis, [(i, (i + by) % size) for i in range(size)])


def window(
    ginv,
    start_hist,
    gcap,
    incoming,
    lnode,
    ladm,
    cnode,
    ccount,
    cstate,
    setpoint_flow,
    crate,
    climit,
    pnode,
    padm,
    pvolt,
):
    nodes = ginv.shape[0]
    lines = lnode.shape[0]
    convs = cnode.shape[0]
    index = jnp.concatenate([lnode, cnode, pnode])
    onehot = (jnp.arange(nodes, dtype=jnp.int32)[:, None] == index[None, :]).astype(jnp.float32)
    picker = onehot.T
    live = (jnp.arange(convs, dtype=jnp.int32) < ccount)[:, None]
    angles = jnp.arange(1, STEPS + 1, dtype=jnp.float32) * jnp.float32(2.0 * math.pi / STEPS)
    limit = climit[:, None]
    slew_limit = crate[:, None]

    def advance(carry, inputs):
        hist_now, inverter_axial_part, inverter_normal_part, acc_re, acc_im = carry
        inward, angle = inputs
        angle_cos_factor = jnp.cos(angle)
        angle_sin_factor = jnp.sin(angle)
        drive = jnp.where(
            live,
            inverter_axial_part * angle_cos_factor - inverter_normal_part * angle_sin_factor,
            0.0,
        )
        source = padm[:, None] * (pvolt[0] * angle_cos_factor - pvolt[1] * angle_sin_factor)
        stacked = jnp.concatenate([inward, drive, source], axis=0)
        right = hist_now + jnp.dot(onehot, stacked, precision=HIGHEST)
        volt = jnp.dot(ginv, right, precision=HIGHEST)
        probe = jnp.dot(picker, volt, precision=HIGHEST)
        at_line = probe[:lines]
        inverter_emf = probe[lines : lines + convs]
        at_port = probe[lines + convs :]
        outward = 2.0 * ladm[:, None] * at_line - inward
        flow = source - padm[:, None] * at_port
        acc_re = acc_re + flow * angle_cos_factor
        acc_im = acc_im - flow * angle_sin_factor
        unclipped_axial_part = (
            inverter_axial_part
            + slew_limit * (setpoint_flow[0] - inverter_axial_part)
            - SAG_FACTOR * inverter_emf * angle_cos_factor
        )
        unclipped_normal_part = (
            inverter_normal_part
            + slew_limit * (setpoint_flow[1] - inverter_normal_part)
            + SAG_FACTOR * inverter_emf * angle_sin_factor
        )
        inverter_axial_part = jnp.where(
            live, limit * jnp.tanh(unclipped_axial_part / limit), inverter_axial_part
        )
        inverter_normal_part = jnp.where(
            live, limit * jnp.tanh(unclipped_normal_part / limit), inverter_normal_part
        )
        hist_now = 2.0 * gcap[:, None] * volt - hist_now
        return ((hist_now, inverter_axial_part, inverter_normal_part, acc_re, acc_im), outward)

    zeros = jnp.zeros(pvolt.shape[1:], dtype=jnp.float32)
    carry = (start_hist, cstate[0], cstate[1], zeros, zeros)
    carry, outward = lax.scan(advance, carry, (incoming, angles))
    hist_end, inverter_axial_part, inverter_normal_part, acc_re, acc_im = carry
    current = jnp.stack([acc_re, acc_im]) * jnp.float32(2.0 / STEPS)
    return (outward, hist_end, jnp.stack([inverter_axial_part, inverter_normal_part]), current)


def per_device(
    conductance_inverse,
    cap_history,
    cap_conductance,
    wave_history,
    line_partner,
    line_node,
    line_delay,
    line_admittance,
    conv_node,
    conv_count,
    conv_state,
    conv_reference,
    conv_rate,
    conv_limit,
    port_node,
    port_admittance,
    port_voltage_prev,
    port_bus,
    transfer_impedance,
):
    subnets = lax.axis_size(("area", "row"))
    own = lax.axis_index(("area", "row"))
    history = wave_history[0]
    lines = history.shape[1]
    partner = line_partner[0]
    offset = (partner - own) % subnets
    signed = jnp.where(offset > subnets // 2, offset - subnets, offset)
    remote = (jnp.arange(lines, dtype=jnp.int32) + lines // 2) % lines
    combined = jnp.zeros(history.shape, jnp.float32)
    for reach in (1, -1, 2, -2):
        count = NEAR if abs(reach) == 1 else lines // 2 - NEAR
        sending = signed == reach
        order = jnp.argsort(jnp.where(sending, 0, 1), stable=True)[:count]
        packed = jnp.take(history, order, axis=1)
        arrived = from_behind(packed, ("area", "row"), reach)
        rank = jnp.cumsum(sending.astype(jnp.int32)) - 1
        slot = jnp.clip(rank[remote], 0, count - 1)
        picked = jnp.take(arrived, slot, axis=1)
        combined = combined + jnp.where((signed == -reach)[None, :, None], picked, 0.0)
    delay = line_delay[0]
    where_now = jnp.arange(STEPS, dtype=jnp.int32)[:, None] - delay[None, :] + HIST
    select = (where_now[:, None, :] == jnp.arange(HIST, dtype=jnp.int32)[None, :, None]).astype(
        jnp.float32
    )
    incoming = jnp.einsum("thl,hlc->tlc", select, combined, precision=HIGHEST)
    outward, hist_end, conv_out, current = window(
        conductance_inverse[0],
        cap_history[0],
        cap_conductance[0],
        incoming,
        line_node[0],
        line_admittance[0],
        conv_node[0],
        conv_count[0],
        conv_state[0],
        conv_reference[0],
        conv_rate[0],
        conv_limit[0],
        port_node[0],
        port_admittance[0],
        port_voltage_prev[:, 0],
    )
    bus_rows = transfer_impedance.shape[1]
    cases = current.shape[2]
    piece = lax.all_gather(current[:, None], "row", axis=1, tiled=True)
    members = piece.shape[1]
    ports = piece.shape[2]
    flat = piece.reshape(2, members * ports, cases)
    real = jnp.dot(transfer_impedance[0], flat[0], precision=HIGHEST) - jnp.dot(
        transfer_impedance[1], flat[1], precision=HIGHEST
    )
    imag = jnp.dot(transfer_impedance[0], flat[1], precision=HIGHEST) + jnp.dot(
        transfer_impedance[1], flat[0], precision=HIGHEST
    )
    partial_bus = jnp.stack([real, imag])
    bus_voltage = lax.psum(partial_bus, "area")
    first_row = lax.axis_index("row") * bus_rows
    local_bus = (port_bus - first_row).reshape(-1)
    pick_rows = (local_bus[:, None] == jnp.arange(bus_rows, dtype=jnp.int32)[None, :]).astype(
        jnp.float32
    )
    gathered = jnp.einsum("jb,xbc->xjc", pick_rows, bus_voltage, precision=HIGHEST)
    gathered = gathered.reshape(2, port_bus.shape[0], port_bus.shape[1], cases)
    port_voltage = lax.psum_scatter(gathered, "row", scatter_dimension=1, tiled=True)
    return (outward[None], hist_end[None], conv_out[None], bus_voltage, port_voltage)


def solution(mesh):
    placed = (
        P(("area", "row"), None, None),
        P(("area", "row"), None, None),
        P(("area", "row"), None),
        P(("area", "row"), None, None, None),
        P(("area", "row"), None),
        P(("area", "row"), None),
        P(("area", "row"), None),
        P(("area", "row"), None),
        P(("area", "row"), None),
        P(("area", "row")),
        P(("area", "row"), None, None, None),
        P(("area", "row"), None, None, None),
        P(("area", "row"), None),
        P(("area", "row"), None),
        P(("area", "row"), None),
        P(("area", "row"), None),
        P(None, ("area", "row"), None, None),
        P("area", None),
        P(None, "row", "area"),
    )
    return jax.shard_map(
        per_device,
        mesh=mesh,
        in_specs=placed,
        out_specs=(
            P(("area", "row"), None, None, None),
            P(("area", "row"), None, None),
            P(("area", "row"), None, None, None),
            P(None, "row", None),
            P(None, ("area", "row"), None, None),
        ),
        check_vma=False,
    )
```

profile of v0, /device:TPU:0, one launch (start us, length us, event | category | flops | bytes accessed | tf_op | source)
XLA Modules:
  0.0 522.5 jit_solution(1617881758800676381)
XLA Ops:
  40.6 254.0 %while.23 = (s32[]{:T(128)}, f32[1024,128]{0,1:T(8,128)S(1)}, f32[64,128]{1,0:T(8,128)S(1)}, f32[64,128]{1,0:T(8,128)S(1)}, f32[8,128]{1,0:T(8,128)S(1)}, /*inde...) while((s32[]{:T(128)}, f32[1024,128]{0,1:T(8,128)S(1)}, ...), condition=%wide.region_9.14_spmd.clone.clone.clone, body=%wide.region_8.13_spmd.clone.clone.clone.sunk | while | flops 1938803712 | bytes 8437999 | solution.py:90
  45.1 6.7 %bitcast_subtract_fusion.4 = (f32[1024,128]{0,1:T(8,128)S(1)}, f32[128,1024]{1,0:T(8,128)S(1)}) fusion(f32[1024,128]{0,1:T(8,128)S(1)} %get-tuple-element.591, f32[1024]{0:T(1024)S(1)} %bitcast.217, f32[1024,128]{0,1:T(8,128)S(1)} %fusion.99, f32[1024,1024]{1,0:T(8,128)} %get-tuple-element.624), kind=kOutput, calls=%fused_computation.18.clone.1 | convolution fusion | flops 1610874880 | bytes 6295552 | tf_op jit(solution)/shard_map/while/body/eval_jaxpr/dot_general | solution.py:60
  57.8 6.7 %bitcast_subtract_fusion.4 = (f32[1024,128]{0,1:T(8,128)S(1)}, f32[128,1024]{1,0:T(8,128)S(1)}) fusion(f32[1024,128]{0,1:T(8,128)S(1)} %get-tuple-element.591, f32[1024]{0:T(1024)S(1)} %bitcast.217, f32[1024,128]{0,1:T(8,128)S(1)} %fusion.99, f32[1024,1024]{1,0:T(8,128)} %get-tuple-element.624), kind=kOutput, calls=%fused_computation.18.clone.1 | convolution fusion | flops 1610874880 | bytes 6295552 | tf_op jit(solution)/shard_map/while/body/eval_jaxpr/dot_general | solution.py:60
  70.5 6.7 %bitcast_subtract_fusion.4 = (f32[1024,128]{0,1:T(8,128)S(1)}, f32[128,1024]{1,0:T(8,128)S(1)}) fusion(f32[1024,128]{0,1:T(8,128)S(1)} %get-tuple-element.591, f32[1024]{0:T(1024)S(1)} %bitcast.217, f32[1024,128]{0,1:T(8,128)S(1)} %fusion.99, f32[1024,1024]{1,0:T(8,128)} %get-tuple-element.624), kind=kOutput, calls=%fused_computation.18.clone.1 | convolution fusion | flops 1610874880 | bytes 6295552 | tf_op jit(solution)/shard_map/while/body/eval_jaxpr/dot_general | solution.py:60
  83.2 6.7 %bitcast_subtract_fusion.4 = (f32[1024,128]{0,1:T(8,128)S(1)}, f32[128,1024]{1,0:T(8,128)S(1)}) fusion(f32[1024,128]{0,1:T(8,128)S(1)} %get-tuple-element.591, f32[1024]{0:T(1024)S(1)} %bitcast.217, f32[1024,128]{0,1:T(8,128)S(1)} %fusion.99, f32[1024,1024]{1,0:T(8,128)} %get-tuple-element.624), kind=kOutput, calls=%fused_computation.18.clone.1 | convolution fusion | flops 1610874880 | bytes 6295552 | tf_op jit(solution)/shard_map/while/body/eval_jaxpr/dot_general | solution.py:60
  95.9 6.7 %bitcast_subtract_fusion.4 = (f32[1024,128]{0,1:T(8,128)S(1)}, f32[128,1024]{1,0:T(8,128)S(1)}) fusion(f32[1024,128]{0,1:T(8,128)S(1)} %get-tuple-element.591, f32[1024]{0:T(1024)S(1)} %bitcast.217, f32[1024,128]{0,1:T(8,128)S(1)} %fusion.99, f32[1024,1024]{1,0:T(8,128)} %get-tuple-element.624), kind=kOutput, calls=%fused_computation.18.clone.1 | convolution fusion | flops 1610874880 | bytes 6295552 | tf_op jit(solution)/shard_map/while/body/eval_jaxpr/dot_general | solution.py:60
  108.6 6.7 %bitcast_subtract_fusion.4 = (f32[1024,128]{0,1:T(8,128)S(1)}, f32[128,1024]{1,0:T(8,128)S(1)}) fusion(f32[1024,128]{0,1:T(8,128)S(1)} %get-tuple-element.591, f32[1024]{0:T(1024)S(1)} %bitcast.217, f32[1024,128]{0,1:T(8,128)S(1)} %fusion.99, f32[1024,1024]{1,0:T(8,128)} %get-tuple-element.624), kind=kOutput, calls=%fused_computation.18.clone.1 | convolution fusion | flops 1610874880 | bytes 6295552 | tf_op jit(solution)/shard_map/while/body/eval_jaxpr/dot_general | solution.py:60
  121.3 6.7 %bitcast_subtract_fusion.4 = (f32[1024,128]{0,1:T(8,128)S(1)}, f32[128,1024]{1,0:T(8,128)S(1)}) fusion(f32[1024,128]{0,1:T(8,128)S(1)} %get-tuple-element.591, f32[1024]{0:T(1024)S(1)} %bitcast.217, f32[1024,128]{0,1:T(8,128)S(1)} %fusion.99, f32[1024,1024]{1,0:T(8,128)} %get-tuple-element.624), kind=kOutput, calls=%fused_computation.18.clone.1 | convolution fusion | flops 1610874880 | bytes 6295552 | tf_op jit(solution)/shard_map/while/body/eval_jaxpr/dot_general | solution.py:60
  134.0 6.7 %bitcast_subtract_fusion.4 = (f32[1024,128]{0,1:T(8,128)S(1)}, f32[128,1024]{1,0:T(8,128)S(1)}) fusion(f32[1024,128]{0,1:T(8,128)S(1)} %get-tuple-element.591, f32[1024]{0:T(1024)S(1)} %bitcast.217, f32[1024,128]{0,1:T(8,128)S(1)} %fusion.99, f32[1024,1024]{1,0:T(8,128)} %get-tuple-element.624), kind=kOutput, calls=%fused_computation.18.clone.1 | convolution fusion | flops 1610874880 | bytes 6295552 | tf_op jit(solution)/shard_map/while/body/eval_jaxpr/dot_general | solution.py:60
  146.7 6.7 %bitcast_subtract_fusion.4 = (f32[1024,128]{0,1:T(8,128)S(1)}, f32[128,1024]{1,0:T(8,128)S(1)}) fusion(f32[1024,128]{0,1:T(8,128)S(1)} %get-tuple-element.591, f32[1024]{0:T(1024)S(1)} %bitcast.217, f32[1024,128]{0,1:T(8,128)S(1)} %fusion.99, f32[1024,1024]{1,0:T(8,128)} %get-tuple-element.624), kind=kOutput, calls=%fused_computation.18.clone.1 | convolution fusion | flops 1610874880 | bytes 6295552 | tf_op jit(solution)/shard_map/while/body/eval_jaxpr/dot_general | solution.py:60
  159.4 6.7 %bitcast_subtract_fusion.4 = (f32[1024,128]{0,1:T(8,128)S(1)}, f32[128,1024]{1,0:T(8,128)S(1)}) fusion(f32[1024,128]{0,1:T(8,128)S(1)} %get-tuple-element.591, f32[1024]{0:T(1024)S(1)} %bitcast.217, f32[1024,128]{0,1:T(8,128)S(1)} %fusion.99, f32[1024,1024]{1,0:T(8,128)} %get-tuple-element.624), kind=kOutput, calls=%fused_computation.18.clone.1 | convolution fusion | flops 1610874880 | bytes 6295552 | tf_op jit(solution)/shard_map/while/body/eval_jaxpr/dot_general | solution.py:60
  172.1 6.7 %bitcast_subtract_fusion.4 = (f32[1024,128]{0,1:T(8,128)S(1)}, f32[128,1024]{1,0:T(8,128)S(1)}) fusion(f32[1024,128]{0,1:T(8,128)S(1)} %get-tuple-element.591, f32[1024]{0:T(1024)S(1)} %bitcast.217, f32[1024,128]{0,1:T(8,128)S(1)} %fusion.99, f32[1024,1024]{1,0:T(8,128)} %get-tuple-element.624), kind=kOutput, calls=%fused_computation.18.clone.1 | convolution fusion | flops 1610874880 | bytes 6295552 | tf_op jit(solution)/shard_map/while/body/eval_jaxpr/dot_general | solution.py:60
  184.8 6.7 %bitcast_subtract_fusion.4 = (f32[1024,128]{0,1:T(8,128)S(1)}, f32[128,1024]{1,0:T(8,128)S(1)}) fusion(f32[1024,128]{0,1:T(8,128)S(1)} %get-tuple-element.591, f32[1024]{0:T(1024)S(1)} %bitcast.217, f32[1024,128]{0,1:T(8,128)S(1)} %fusion.99, f32[1024,1024]{1,0:T(8,128)} %get-tuple-element.624), kind=kOutput, calls=%fused_computation.18.clone.1 | convolution fusion | flops 1610874880 | bytes 6295552 | tf_op jit(solution)/shard_map/while/body/eval_jaxpr/dot_general | solution.py:60
  197.5 6.7 %bitcast_subtract_fusion.4 = (f32[1024,128]{0,1:T(8,128)S(1)}, f32[128,1024]{1,0:T(8,128)S(1)}) fusion(f32[1024,128]{0,1:T(8,128)S(1)} %get-tuple-element.591, f32[1024]{0:T(1024)S(1)} %bitcast.217, f32[1024,128]{0,1:T(8,128)S(1)} %fusion.99, f32[1024,1024]{1,0:T(8,128)} %get-tuple-element.624), kind=kOutput, calls=%fused_computation.18.clone.1 | convolution fusion | flops 1610874880 | bytes 6295552 | tf_op jit(solution)/shard_map/while/body/eval_jaxpr/dot_general | solution.py:60
  210.2 6.7 %bitcast_subtract_fusion.4 = (f32[1024,128]{0,1:T(8,128)S(1)}, f32[128,1024]{1,0:T(8,128)S(1)}) fusion(f32[1024,128]{0,1:T(8,128)S(1)} %get-tuple-element.591, f32[1024]{0:T(1024)S(1)} %bitcast.217, f32[1024,128]{0,1:T(8,128)S(1)} %fusion.99, f32[1024,1024]{1,0:T(8,128)} %get-tuple-element.624), kind=kOutput, calls=%fused_computation.18.clone.1 | convolution fusion | flops 1610874880 | bytes 6295552 | tf_op jit(solution)/shard_map/while/body/eval_jaxpr/dot_general | solution.py:60
  222.9 6.7 %bitcast_subtract_fusion.4 = (f32[1024,128]{0,1:T(8,128)S(1)}, f32[128,1024]{1,0:T(8,128)S(1)}) fusion(f32[1024,128]{0,1:T(8,128)S(1)} %get-tuple-element.591, f32[1024]{0:T(1024)S(1)} %bitcast.217, f32[1024,128]{0,1:T(8,128)S(1)} %fusion.99, f32[1024,1024]{1,0:T(8,128)} %get-tuple-element.624), kind=kOutput, calls=%fused_computation.18.clone.1 | convolution fusion | flops 1610874880 | bytes 6295552 | tf_op jit(solution)/shard_map/while/body/eval_jaxpr/dot_general | solution.py:60
  235.6 6.7 %bitcast_subtract_fusion.4 = (f32[1024,128]{0,1:T(8,128)S(1)}, f32[128,1024]{1,0:T(8,128)S(1)}) fusion(f32[1024,128]{0,1:T(8,128)S(1)} %get-tuple-element.591, f32[1024]{0:T(1024)S(1)} %bitcast.217, f32[1024,128]{0,1:T(8,128)S(1)} %fusion.99, f32[1024,1024]{1,0:T(8,128)} %get-tuple-element.624), kind=kOutput, calls=%fused_computation.18.clone.1 | convolution fusion | flops 1610874880 | bytes 6295552 | tf_op jit(solution)/shard_map/while/body/eval_jaxpr/dot_general | solution.py:60
  248.3 6.7 %bitcast_subtract_fusion.4 = (f32[1024,128]{0,1:T(8,128)S(1)}, f32[128,1024]{1,0:T(8,128)S(1)}) fusion(f32[1024,128]{0,1:T(8,128)S(1)} %get-tuple-element.591, f32[1024]{0:T(1024)S(1)} %bitcast.217, f32[1024,128]{0,1:T(8,128)S(1)} %fusion.99, f32[1024,1024]{1,0:T(8,128)} %get-tuple-element.624), kind=kOutput, calls=%fused_computation.18.clone.1 | convolution fusion | flops 1610874880 | bytes 6295552 | tf_op jit(solution)/shard_map/while/body/eval_jaxpr/dot_general | solution.py:60
  261.0 6.7 %bitcast_subtract_fusion.4 = (f32[1024,128]{0,1:T(8,128)S(1)}, f32[128,1024]{1,0:T(8,128)S(1)}) fusion(f32[1024,128]{0,1:T(8,128)S(1)} %get-tuple-element.591, f32[1024]{0:T(1024)S(1)} %bitcast.217, f32[1024,128]{0,1:T(8,128)S(1)} %fusion.99, f32[1024,1024]{1,0:T(8,128)} %get-tuple-element.624), kind=kOutput, calls=%fused_computation.18.clone.1 | convolution fusion | flops 1610874880 | bytes 6295552 | tf_op jit(solution)/shard_map/while/body/eval_jaxpr/dot_general | solution.py:60
  273.7 6.7 %bitcast_subtract_fusion.4 = (f32[1024,128]{0,1:T(8,128)S(1)}, f32[128,1024]{1,0:T(8,128)S(1)}) fusion(f32[1024,128]{0,1:T(8,128)S(1)} %get-tuple-element.591, f32[1024]{0:T(1024)S(1)} %bitcast.217, f32[1024,128]{0,1:T(8,128)S(1)} %fusion.99, f32[1024,1024]{1,0:T(8,128)} %get-tuple-element.624), kind=kOutput, calls=%fused_computation.18.clone.1 | convolution fusion | flops 1610874880 | bytes 6295552 | tf_op jit(solution)/shard_map/while/body/eval_jaxpr/dot_general | solution.py:60
  286.4 6.7 %bitcast_subtract_fusion.4 = (f32[1024,128]{0,1:T(8,128)S(1)}, f32[128,1024]{1,0:T(8,128)S(1)}) fusion(f32[1024,128]{0,1:T(8,128)S(1)} %get-tuple-element.591, f32[1024]{0:T(1024)S(1)} %bitcast.217, f32[1024,128]{0,1:T(8,128)S(1)} %fusion.99, f32[1024,1024]{1,0:T(8,128)} %get-tuple-element.624), kind=kOutput, calls=%fused_computation.18.clone.1 | convolution fusion | flops 1610874880 | bytes 6295552 | tf_op jit(solution)/shard_map/while/body/eval_jaxpr/dot_general | solution.py:60
  315.0 177.5 %all-reduce.3.cloned.1.call-done = f32[2,5120,128]{1,2,0:T(8,128)} async-done(((f32[2,5120,128]{1,2,0:T(8,128)}), f32[2,5120,128]{1,2,0:T(8,128)}) %all-reduce.3.cloned.1.call-update) | async-done | bytes 5242896 | tf_op jit(solution)/shard_map/psum | solution.py:172
  497.7 10.9 %all-reduce = f32[2,4,8,128]{3,2,1,0:T(8,128)S(1)} all-reduce(f32[2,4,8,128]{3,2,1,0:T(8,128)S(1)} %convolution_bitcast_fusion.3), channel_id=2, replica_groups=mesh['area'=8,'row'=4] {'row'}, use_global_device_ids=true, to_apply=%region_11.16.clone | all-reduce | flops 8192 | bytes 65536
  509.8 5.9 %copy.50 = f32[2,5120,128]{2,1,0:T(8,128)} copy(f32[2,5120,128]{1,2,0:T(8,128)} %all-reduce.3.cloned.1.call-done) | data formatting | bytes 10485760
  (362 shorter events, 149.4 us)
Async XLA Ops:
  7.2 19.4 %copy-start.11 = (s32[1,32]{1,0:T(1,128)S(1)}, s32[1,32]{1,0:T(1,128)}, u32[]{:S(2)}) copy-start(s32[1,32]{1,0:T(1,128)} %param.33) | copy-start | bytes 388
  7.2 19.6 %copy-start.10 = (s32[1,32]{1,0:T(1,128)S(1)}, s32[1,32]{1,0:T(1,128)}, u32[]{:S(2)}) copy-start(s32[1,32]{1,0:T(1,128)} %param.35) | copy-start | bytes 388
  7.2 485.3 %all-reduce.3.cloned.1.call-start = ((), (), s32[]{:S(2)}) async-start(), calls=%async_computation | async-start | bytes 10485760 | tf_op jit(solution)/shard_map/psum | solution.py:172
  11.6 18.9 %copy-start.5 = (f32[1,2,64,128]{3,2,1,0:T(8,128)S(1)}, f32[1,2,64,128]{3,2,1,0:T(8,128)}, u32[]{:S(2)}) copy-start(f32[1,2,64,128]{3,2,1,0:T(8,128)} %param.39) | copy-start | bytes 196612
  11.7 19.8 %collective-permute-start.2 = (f32[40,4,128]{2,0,1:T(8,128)S(1)}, f32[40,4,128]{2,0,1:T(8,128)S(1)}, u32[]{:S(2)}, u32[]{:S(2)}) collective-permute-start(f32[40,4,128]{2,0,1:T(8,128)S(1)} %select_bitcast_fusion.3), channel_id=1, source_target_pairs={{0,2},{1,3},{2,4},{3,5},{4,6},{5,7},{6,8},{7,9},{8,10},{9,11},{10,... | collective-permute-start | bytes 245768 | tf_op jit(solution)/shard_map/ppermute | solution.py:16
  16.3 14.3 %copy-start.3 = (f32[1,1024,128]{2,1,0:T(8,128)S(1)}, f32[1,1024,128]{2,1,0:T(8,128)}, u32[]{:S(2)}) copy-start(f32[1,1024,128]{2,1,0:T(8,128)} %param.30) | copy-start | bytes 1572868
  17.0 13.9 %collective-permute-start.3 = (f32[40,4,128]{2,0,1:T(8,128)S(1)}, f32[40,4,128]{2,0,1:T(8,128)S(1)}, u32[]{:S(2)}, u32[]{:S(2)}) collective-permute-start(f32[40,4,128]{2,0,1:T(8,128)S(1)} %select_bitcast_fusion.2), channel_id=1, source_target_pairs={{0,30},{1,31},{2,0},{3,1},{4,2},{5,3},{6,4},{7,5},{8,6},{9,7},{10,... | collective-permute-start | bytes 245768 | tf_op jit(solution)/shard_map/ppermute | solution.py:16
  23.1 7.7 %copy-start.12 = (s32[1,8]{1,0:T(1,128)S(1)}, s32[1,8]{1,0:T(1,128)}, u32[]{:S(2)}) copy-start(s32[1,8]{1,0:T(1,128)} %param.43) | copy-start | bytes 100
  23.1 7.7 %copy-start.13 = (s32[1,64]{1,0:T(1,128)S(1)}, s32[1,64]{1,0:T(1,128)}, u32[]{:S(2)}) copy-start(s32[1,64]{1,0:T(1,128)} %param.37) | copy-start | bytes 772
  23.2 7.6 %copy-start.14 = (s32[1,32]{1,0:T(1,128)S(1)}, s32[1,32]{1,0:T(1,128)}, u32[]{:S(2)}) copy-start(s32[1,32]{1,0:T(1,128)} %param.34) | copy-start | bytes 388
  23.3 13.2 %collective-permute-start.1 = (f32[40,12,128]{2,0,1:T(8,128)S(1)}, f32[40,12,128]{2,0,1:T(8,128)S(1)}, u32[]{:S(2)}, u32[]{:S(2)}) collective-permute-start(f32[40,12,128]{2,0,1:T(8,128)S(1)} %select_bitcast_fusion), channel_id=1, source_target_pairs={{0,31},{1,0},{2,1},{3,2},{4,3},{5,4},{6,5},{7,6},{8,7},{9,8},{10,9... | collective-permute-start | bytes 737288 | tf_op jit(solution)/shard_map/ppermute | solution.py:16
  26.5 9.3 %collective-permute-start = (f32[40,12,128]{2,0,1:T(8,128)S(1)}, f32[40,12,128]{2,0,1:T(8,128)S(1)}, u32[]{:S(2)}, u32[]{:S(2)}) collective-permute-start(f32[40,12,128]{2,0,1:T(8,128)S(1)} %select_bitcast_fusion.1), channel_id=1, source_target_pairs={{0,1},{1,2},{2,3},{3,4},{4,5},{5,6},{6,7},{7,8},{8,9},{9,10},{10,1... | collective-permute-start | bytes 737288 | tf_op jit(solution)/shard_map/ppermute | solution.py:16
  36.4 4.2 copy-start.1
  36.4 4.2 copy-start.2
  36.4 4.2 copy-start.4
  36.4 4.2 copy-start.6
  36.4 4.2 copy-start.7
  36.4 4.2 copy-start.8
  36.4 4.2 copy-start.15
  40.6 259.4 %copy-start = (f32[2,5120,32]{1,2,0:T(8,128)S(1)}, f32[2,5120,32]{1,2,0:T(8,128)}, u32[]{:S(2)}) copy-start(f32[2,5120,32]{1,2,0:T(8,128)} %param.47) | copy-start | bytes 3932164
  312.0 0.7 copy-start.9
  312.0 0.8 copy-start.16
Sparse Core Ops, SparseCore 0:
  312.1 180.2 all-reduce.2
where the time goes:
time: 525 us; the launch traced here: 523 us
  waiting for transfers between devices  181 us (34%)
  matrix products  178 us (34%)
  local copies, waits for them, and re-layouts  49.6 us (9%)
  other arithmetic  45.4 us (9%)
  loops' own time  29.9 us (6%)
  blocking collectives  16.3 us (3%)
  between operations  14.6 us (3%)
  starting transfers between devices  8.01 us (2%)
    psum x1, waiting for transfers between devices, per_device(): bus_voltage = lax.psum(partial_bus, 'area')  177 us
    dot_general x20, matrix products, advance(): volt = jnp.dot(ginv, right, precision=HIGHEST)  134 us
    dynamic_slice x40, local copies, waits for them, and re-layouts, window(): carry, outward = lax.scan(advance, carry, (incoming, angles))  30 us
    another operation x1, loops' own time, window(): carry, outward = lax.scan(advance, carry, (incoming, angles))  29.9 us
    dynamic_update_slice x20, other arithmetic, window(): carry, outward = lax.scan(advance, carry, (incoming, angles))  13.7 us
    dot_general x20, matrix products, advance(): probe = jnp.dot(picker, volt, precision=HIGHEST)  13.4 us
    broadcast_in_dim x20, other arithmetic, advance(): jnp.where(live, inverter_axial_part * angle_cos_factor - inverter_normal_...  13.1 us
    dot_general x20, matrix products, advance(): right = hist_now + jnp.dot(onehot, stacked, precision=HIGHEST)  12.9 us
  transfers between devices with their start and end apart: 5, of which 2 were waited for; matrix products, arithmetic and copies ran while one was open for 3% of the time, Pallas kernels for 0%

commit v1 on v0

--- a/solution.py
+++ b/solution.py
@@ -9,6 +9,19 @@
 NEAR = 12
 HIGHEST = lax.Precision.HIGHEST
 SAG_FACTOR = 0.3
+
+
+def track_node(xx):
+    a_name = "area"
+    parts_n = lax.axis_size(a_name)
+    clean, newest = (xx, 0)
+    while 1 << newest < parts_n:
+        a_next = lax.ppermute(
+            clean, axis_name=a_name, perm=[(kk, kk ^ 1 << newest) for kk in range(parts_n)]
+        )
+        clean = clean + a_next
+        newest = newest + 1
+    return clean
 
 
 def from_behind(x, axis, by):
@@ -169,7 +182,7 @@
         transfer_impedance[1], flat[0], precision=HIGHEST
     )
     partial_bus = jnp.stack([real, imag])
-    bus_voltage = lax.psum(partial_bus, "area")
+    bus_voltage = track_node(partial_bus)
     first_row = lax.axis_index("row") * bus_rows
     local_bus = (port_bus - first_row).reshape(-1)
     pick_rows = (local_bus[:, None] == jnp.arange(bus_rows, dtype=jnp.int32)[None, :]).astype(

time: 525 us -> 818 us (1.56)
  waiting for transfers between devices: 181 us -> 452 us
  other arithmetic: 45.4 us -> 61.5 us
  local copies, waits for them, and re-layouts: 49.6 us -> 63.4 us
  between operations: 14.6 us -> 1.06 us
    ppermute x0 -> x3, waiting for transfers between devices: none -> 452 us  [track_node(): lax.ppermute(clean, axis_name=a_name, perm=[(kk, kk ^ 1 << newest) for kk...]
    psum x1 -> x0, waiting for transfers between devices: 177 us -> none  [per_device(): bus_voltage = lax.psum(partial_bus, 'area')]
    add x0 -> x3, other arithmetic: none -> 14.1 us  [track_node(): clean = clean + a_next]
    dynamic_slice x40, local copies, waits for them, and re-layouts: 30 us -> 43.9 us  [window(): carry, outward = lax.scan(advance, carry, (incoming, angles))]
  transfers between devices with their start and end apart: 5 -> 7, of which waited for: 2 -> 3; matrix products, arithmetic and copies ran while one was open for 3% -> 2% of each run, Pallas kernels for 0% -> 0%
where the time goes in v1:
time: 818 us; the launch traced here: 816 us
  waiting for transfers between devices  452 us (55%)
  matrix products  178 us (22%)
  local copies, waits for them, and re-layouts  63.4 us (8%)
  other arithmetic  61.5 us (8%)
  loops' own time  30.3 us (4%)
  blocking collectives  15.6 us (2%)
  starting transfers between devices  13.9 us (2%)
    ppermute x3, waiting for transfers between devices, track_node(): lax.ppermute(clean, axis_name=a_name, perm=[(kk, kk ^ 1 << newest) for kk...  452 us
    dot_general x20, matrix products, advance(): volt = jnp.dot(ginv, right, precision=HIGHEST)  134 us
    dynamic_slice x40, local copies, waits for them, and re-layouts, window(): carry, outward = lax.scan(advance, carry, (incoming, angles))  43.9 us
    another operation x1, loops' own time, window(): carry, outward = lax.scan(advance, carry, (incoming, angles))  30.3 us
  transfers between devices with their start and end apart: 7, of which 3 were waited for; matrix products, arithmetic and copies ran while one was open for 2% of the time, Pallas kernels for 0%

profile of v1, /device:TPU:0, one launch (start us, length us, event | category | flops | bytes accessed | tf_op | source)
XLA Modules:
  0.0 815.8 jit_solution(4600437952398727485)
XLA Ops:
  5.7 7.0 collective-permute-start.3
  38.8 268.4 %while.23 = (s32[]{:T(128)}, f32[1024,128]{0,1:T(8,128)S(1)}, f32[64,128]{1,0:T(8,128)S(1)}, f32[64,128]{1,0:T(8,128)S(1)}, f32[8,128]{1,0:T(8,128)S(1)}, /*inde...) while((s32[]{:T(128)}, f32[1024,128]{0,1:T(8,128)S(1)}, ...), condition=%wide.region_9.14_spmd.clone.clone.clone, body=%wide.region_8.13_spmd.clone.clone.clone.sunk | while | flops 1938803712 | bytes 8439591 | solution.py:103
  44.0 6.7 bitcast_subtract_fusion.4
  57.4 6.7 bitcast_subtract_fusion.4
  84.3 6.7 bitcast_subtract_fusion.4
  97.7 6.7 bitcast_subtract_fusion.4
  111.1 6.7 bitcast_subtract_fusion.4
  124.5 6.7 bitcast_subtract_fusion.4
  137.9 6.7 bitcast_subtract_fusion.4
  164.7 6.7 bitcast_subtract_fusion.4
  178.2 6.7 bitcast_subtract_fusion.4
  191.6 6.7 bitcast_subtract_fusion.4
  205.0 6.7 bitcast_subtract_fusion.4
  218.4 6.7 bitcast_subtract_fusion.4
  245.2 6.7 bitcast_subtract_fusion.4
  258.6 6.7 bitcast_subtract_fusion.4
  272.1 6.7 bitcast_subtract_fusion.4
  285.5 6.7 bitcast_subtract_fusion.4
  298.9 6.7 bitcast_subtract_fusion.4
  322.0 115.3 %collective-permute-done.4 = f32[2,5120,128]{1,2,0:T(8,128)S(1)} collective-permute-done((f32[2,5120,128]{1,2,0:T(8,128)S(1)}, f32[2,5120,128]{1,2,0:T(8,128)S(1)}, u32[]{:S(2)}, u32[]{:S(2)}) %collective-permute-start.4) | collective-permute-done | bytes 5242912 | tf_op jit(solution)/shard_map/ppermute | solution.py:19
  438.2 114.5 %collective-permute-done.5 = f32[2,5120,128]{1,2,0:T(8,128)} collective-permute-done((f32[2,5120,128]{1,2,0:T(8,128)S(1)}, f32[2,5120,128]{1,2,0:T(8,128)}, u32[]{:S(2)}, u32[]{:S(2)}) %collective-permute-start.5) | collective-permute-done | bytes 5242912 | tf_op jit(solution)/shard_map/ppermute | solution.py:19
  563.3 222.7 %collective-permute-done.6 = f32[2,5120,128]{1,2,0:T(8,128)} collective-permute-done((f32[2,5120,128]{1,2,0:T(8,128)}, f32[2,5120,128]{1,2,0:T(8,128)}, u32[]{:S(2)}, u32[]{:S(2)}) %collective-permute-start.6) | collective-permute-done | bytes 5242912 | tf_op jit(solution)/shard_map/ppermute | solution.py:19
  786.0 7.2 add.227
  804.3 10.3 %all-reduce = f32[2,4,8,128]{3,2,1,0:T(8,128)S(1)} all-reduce(f32[2,4,8,128]{3,2,1,0:T(8,128)S(1)} %convolution_bitcast_fusion.3), channel_id=2, replica_groups=mesh['area'=8,'row'=4] {'row'}, use_global_device_ids=true, to_apply=%region_10.15.clone | all-reduce | flops 8192 | bytes 65536
  (444 shorter events, 193.3 us)
Async XLA Ops:
  0.6 23.5 %copy-start.11 = (s32[1,32]{1,0:T(1,128)S(1)}, s32[1,32]{1,0:T(1,128)}, u32[]{:S(2)}) copy-start(s32[1,32]{1,0:T(1,128)} %param.33) | copy-start | bytes 388
  0.6 24.3 %copy-start.5 = (f32[1,2,64,128]{3,2,1,0:T(8,128)S(1)}, f32[1,2,64,128]{3,2,1,0:T(8,128)}, u32[]{:S(2)}) copy-start(f32[1,2,64,128]{3,2,1,0:T(8,128)} %param.39) | copy-start | bytes 196612
  0.7 29.6 %copy-start.10 = (s32[1,32]{1,0:T(1,128)S(1)}, s32[1,32]{1,0:T(1,128)}, u32[]{:S(2)}) copy-start(s32[1,32]{1,0:T(1,128)} %param.35) | copy-start | bytes 388
  0.7 30.9 %copy-start.3 = (f32[1,1024,128]{2,1,0:T(8,128)S(1)}, f32[1,1024,128]{2,1,0:T(8,128)}, u32[]{:S(2)}) copy-start(f32[1,1024,128]{2,1,0:T(8,128)} %param.30) | copy-start | bytes 1572868
  0.7 31.7 %copy-start.12 = (s32[1,8]{1,0:T(1,128)S(1)}, s32[1,8]{1,0:T(1,128)}, u32[]{:S(2)}) copy-start(s32[1,8]{1,0:T(1,128)} %param.43) | copy-start | bytes 100
  0.7 31.7 %copy-start.13 = (s32[1,64]{1,0:T(1,128)S(1)}, s32[1,64]{1,0:T(1,128)}, u32[]{:S(2)}) copy-start(s32[1,64]{1,0:T(1,128)} %param.37) | copy-start | bytes 772
  0.7 31.7 %copy-start.14 = (s32[1,32]{1,0:T(1,128)S(1)}, s32[1,32]{1,0:T(1,128)}, u32[]{:S(2)}) copy-start(s32[1,32]{1,0:T(1,128)} %param.34) | copy-start | bytes 388
  5.7 26.7 %collective-permute-start.3 = (f32[40,4,128]{2,0,1:T(8,128)S(1)}, f32[40,4,128]{2,0,1:T(8,128)S(1)}, u32[]{:S(2)}, u32[]{:S(2)}) collective-permute-start(f32[40,4,128]{2,0,1:T(8,128)S(1)} %select_bitcast_fusion.2), channel_id=1, source_target_pairs={{0,30},{1,31},{2,0},{3,1},{4,2},{5,3},{6,4},{7,5},{8,6},{9,7},{10,... | collective-permute-start | bytes 245768 | tf_op jit(solution)/shard_map/ppermute | solution.py:29
  14.9 18.1 %collective-permute-start.2 = (f32[40,4,128]{2,0,1:T(8,128)S(1)}, f32[40,4,128]{2,0,1:T(8,128)S(1)}, u32[]{:S(2)}, u32[]{:S(2)}) collective-permute-start(f32[40,4,128]{2,0,1:T(8,128)S(1)} %select_bitcast_fusion.3), channel_id=1, source_target_pairs={{0,2},{1,3},{2,4},{3,5},{4,6},{5,7},{6,8},{7,9},{8,10},{9,11},{10,... | collective-permute-start | bytes 245768 | tf_op jit(solution)/shard_map/ppermute | solution.py:29
  17.3 16.4 %collective-permute-start.1 = (f32[40,12,128]{2,0,1:T(8,128)S(1)}, f32[40,12,128]{2,0,1:T(8,128)S(1)}, u32[]{:S(2)}, u32[]{:S(2)}) collective-permute-start(f32[40,12,128]{2,0,1:T(8,128)S(1)} %select_bitcast_fusion), channel_id=1, source_target_pairs={{0,31},{1,0},{2,1},{3,2},{4,3},{5,4},{6,5},{7,6},{8,7},{9,8},{10,9... | collective-permute-start | bytes 737288 | tf_op jit(solution)/shard_map/ppermute | solution.py:29
  24.1 10.3 %collective-permute-start = (f32[40,12,128]{2,0,1:T(8,128)S(1)}, f32[40,12,128]{2,0,1:T(8,128)S(1)}, u32[]{:S(2)}, u32[]{:S(2)}) collective-permute-start(f32[40,12,128]{2,0,1:T(8,128)S(1)} %select_bitcast_fusion.1), channel_id=1, source_target_pairs={{0,1},{1,2},{2,3},{3,4},{4,5},{5,6},{6,7},{7,8},{8,9},{9,10},{10,1... | collective-permute-start | bytes 737288 | tf_op jit(solution)/shard_map/ppermute | solution.py:29
  38.7 273.8 %copy-start = (f32[2,5120,32]{1,2,0:T(8,128)S(1)}, f32[2,5120,32]{1,2,0:T(8,128)}, u32[]{:S(2)}) copy-start(f32[2,5120,32]{1,2,0:T(8,128)} %param.47) | copy-start | bytes 3932164
  38.8 12.6 %copy-start.8 = (f32[64,1]{0,1:T(1,128)S(1)}, f32[64,1]{0,1:T(1,128)}, u32[]{:S(2)}) copy-start(f32[64,1]{0,1:T(1,128)} %get-tuple-element.626) | copy-start | bytes 772 | tf_op jit(solution)/shard_map/while
  52.3 12.5 %copy-start.8 = (f32[64,1]{0,1:T(1,128)S(1)}, f32[64,1]{0,1:T(1,128)}, u32[]{:S(2)}) copy-start(f32[64,1]{0,1:T(1,128)} %get-tuple-element.626) | copy-start | bytes 772 | tf_op jit(solution)/shard_map/while
  92.5 12.5 %copy-start.8 = (f32[64,1]{0,1:T(1,128)S(1)}, f32[64,1]{0,1:T(1,128)}, u32[]{:S(2)}) copy-start(f32[64,1]{0,1:T(1,128)} %get-tuple-element.626) | copy-start | bytes 772 | tf_op jit(solution)/shard_map/while
  106.0 12.5 %copy-start.8 = (f32[64,1]{0,1:T(1,128)S(1)}, f32[64,1]{0,1:T(1,128)}, u32[]{:S(2)}) copy-start(f32[64,1]{0,1:T(1,128)} %get-tuple-element.626) | copy-start | bytes 772 | tf_op jit(solution)/shard_map/while
  119.4 12.5 %copy-start.8 = (f32[64,1]{0,1:T(1,128)S(1)}, f32[64,1]{0,1:T(1,128)}, u32[]{:S(2)}) copy-start(f32[64,1]{0,1:T(1,128)} %get-tuple-element.626) | copy-start | bytes 772 | tf_op jit(solution)/shard_map/while
  132.8 12.5 %copy-start.8 = (f32[64,1]{0,1:T(1,128)S(1)}, f32[64,1]{0,1:T(1,128)}, u32[]{:S(2)}) copy-start(f32[64,1]{0,1:T(1,128)} %get-tuple-element.626) | copy-start | bytes 772 | tf_op jit(solution)/shard_map/while
  173.0 12.5 %copy-start.8 = (f32[64,1]{0,1:T(1,128)S(1)}, f32[64,1]{0,1:T(1,128)}, u32[]{:S(2)}) copy-start(f32[64,1]{0,1:T(1,128)} %get-tuple-element.626) | copy-start | bytes 772 | tf_op jit(solution)/shard_map/while
  321.9 115.4 %collective-permute-start.4 = (f32[2,5120,128]{1,2,0:T(8,128)S(1)}, f32[2,5120,128]{1,2,0:T(8,128)S(1)}, u32[]{:S(2)}, u32[]{:S(2)}) collective-permute-start(f32[2,5120,128]{1,2,0:T(8,128)S(1)} %pad_maximum_fusion), channel_id=1, source_target_pairs={{0,4},{4,0},{8,12},{12,8},{16,20},{20,16},{24,28},{28,24},{1,5},{5... | collective-permute-start | bytes 15728648 | tf_op jit(solution)/shard_map/ppermute | solution.py:19
  438.1 122.9 %copy-start.9 = (s32[4,8]{1,0:T(4,128)S(1)}, s32[4,8]{1,0:T(4,128)}, u32[]{:S(2)}) copy-start(s32[4,8]{1,0:T(4,128)} %param.46) | copy-start | bytes 388
  438.1 123.0 %copy-start.16 = (u32[32]{0:T(128)S(1)}, u32[32]{0:T(128)}, u32[]{:S(2)}) copy-start(u32[32]{0:T(128)} %constant.155) | copy-start | bytes 388
  438.1 114.6 %collective-permute-start.5 = (f32[2,5120,128]{1,2,0:T(8,128)S(1)}, f32[2,5120,128]{1,2,0:T(8,128)}, u32[]{:S(2)}, u32[]{:S(2)}) collective-permute-start(f32[2,5120,128]{1,2,0:T(8,128)S(1)} %fusion.80), channel_id=1, source_target_pairs={{0,8},{4,12},{8,0},{12,4},{16,24},{20,28},{24,16},{28,20},{1,9},{5... | collective-permute-start | bytes 15728648 | tf_op jit(solution)/shard_map/ppermute | solution.py:19
  558.8 227.2 %collective-permute-start.6 = (f32[2,5120,128]{1,2,0:T(8,128)}, f32[2,5120,128]{1,2,0:T(8,128)}, u32[]{:S(2)}, u32[]{:S(2)}) collective-permute-start(f32[2,5120,128]{1,2,0:T(8,128)} %fusion.85), channel_id=1, source_target_pairs={{0,16},{4,20},{8,24},{12,28},{16,0},{20,4},{24,8},{28,12},{1,17},{... | collective-permute-start | bytes 15728648 | tf_op jit(solution)/shard_map/ppermute | solution.py:19
  (38 other events, 379.8 us)
